TPU v7x, 32 devices: a whole 2x2x4 slice. The times are simulated.
32 devices in a mesh: tm: 2 (over x), sx: 4 (over z), sy: 4 (over y, core).
Axes of the slice: x: 2, y: 2, z: 4, core: 2. Of those that a mesh axis runs over, the one named last changes fastest.
Arguments:
- heat_source: float32 [8, 64, 64, 128], P('tm', 'sx', 'sy'), may hold values from -8 to 8
- conductivity: float32 [64, 64, 128], P('sx', 'sy'), may hold values from 0.001 to 0.5
- initial_iterate: float32 [8, 64, 64, 128], P('tm', 'sx', 'sy'), may hold values from -6 to 6
Outputs:
- solution: float32 [8, 64, 64, 128], P('tm', 'sx', 'sy')
- residual: float32 [8, 64, 64, 128], P('tm', 'sx', 'sy')
All inputs are finite; a program needn't handle non-finite values.
Results may differ from a plain program's by a relative error of at most 0.000074.
Values sent between devices are 32-bit elements; how exact they have to be, the bound alone decides.
A program may use at most 64 MiB of HBM per device.

v0:
```python
import functools

import jax
import jax.numpy as jnp
from jax import lax
from jax.experimental import pallas as pl
from jax.experimental.pallas import tpu as pltpu
from jax.sharding import PartitionSpec as P

relax_weight = 0.8
keep_weight = 1.0 - relax_weight
MESH = pl.DeviceIdType.MESH

KAPPA, INIT, FIRST, ERR1, ERR2, ERR3, FIX2, FIX1, SUM0, SOL, PART, PAIR, PART2, PAIR2 = range(14)
FIELDS = 14
P_INIT, P_FIRST, P_ERR1, P_ERR2, P_FIX1, P_SUM0, P_SOL = range(7)
XLO, XHI, YLO, YHI = range(4)


def kernel(n_tm, n_sx, n_sy, hs_hbm, k_hbm, in_hbm, sol_hbm, res_hbm, *scratch):
    fields = scratch[:FIELDS]
    yrecv = scratch[FIELDS:2 * FIELDS]
    ysend = scratch[2 * FIELDS:3 * FIELDS]
    (hs, res, before, second, rhs1, rhs2, rhs3, mine, theirs, chain,
     face, coupling, factor, send_sem, recv_sem, tsend, trecv,
     qsend, qrecv, csend, crecv, local) = scratch[3 * FIELDS:]
    steps, nx, ny, nz = hs.shape
    tm, sx, sy = lax.axis_index("tm"), lax.axis_index("sx"), lax.axis_index("sy")
    has = (sx > 0, sx < n_sx - 1, sy > 0, sy < n_sy - 1)
    partner = tm + 1 - 2 * lax.rem(tm, 2)
    even = lax.rem(tm, 2) == 0

    loads = [
        pltpu.make_async_copy(k_hbm, fields[KAPPA].at[0, pl.ds(1, nx)], local.at[0]),
        pltpu.make_async_copy(in_hbm, fields[INIT].at[:, pl.ds(1, nx)], local.at[1]),
        pltpu.make_async_copy(hs_hbm, hs, local.at[2]),
    ]
    for load in loads:
        load.start()

    barrier = pltpu.get_barrier_semaphore()
    greet = [
        (has[XLO], {"sx": sx - 1}), (has[XHI], {"sx": sx + 1}),
        (has[YLO], {"sy": sy - 1}), (has[YHI], {"sy": sy + 1}),
        (tm > 0, {"tm": tm - 1}), (tm < n_tm - 1, {"tm": tm + 1}),
    ]
    if n_tm == 2:
        greet += [
            (has[XLO], {"tm": partner, "sx": sx - 1}), (has[XHI], {"tm": partner, "sx": sx + 1}),
            (has[YLO], {"tm": partner, "sy": sy - 1}), (has[YHI], {"tm": partner, "sy": sy + 1}),
        ]
    if n_tm > 2:
        greet += [(tm > 1, {"tm": tm - 2}), (tm < n_tm - 2, {"tm": tm + 2})]
    count = jnp.int32(0)
    for there, device in greet:
        count = count + jnp.where(there, 1, 0)

        @pl.when(there)
        def _(device=device):
            pl.semaphore_signal(barrier, inc=1, device_id=device, device_id_type=MESH)

    pl.semaphore_wait(barrier, count)

    def face_copy(i, side, pair=False):
        field = fields[i]
        to = i + 1 if pair else i
        land = fields[to]
        if side == XLO:
            if i == INIT:
                src = in_hbm.at[:, pl.ds(0, 1)]
            elif i == KAPPA:
                src = k_hbm.at[pl.ds(0, 1)]
            else:
                src = field.at[:, pl.ds(1, 1)]
            dst, device = land.at[:, pl.ds(nx + 1, 1)], {"sx": sx - 1}
        elif side == XHI:
            if i == INIT:
                src = in_hbm.at[:, pl.ds(nx - 1, 1)]
            elif i == KAPPA:
                src = k_hbm.at[pl.ds(nx - 1, 1)]
            else:
                src = field.at[:, pl.ds(nx, 1)]
            dst, device = land.at[:, pl.ds(0, 1)], {"sx": sx + 1}
        elif side == YLO:
            src, dst, device = ysend[i].at[0], yrecv[to].at[1], {"sy": sy - 1}
        else:
            src, dst, device = ysend[i].at[1], yrecv[to].at[0], {"sy": sy + 1}
        if i == KAPPA and side in (XLO, XHI):
            dst = field.at[0, pl.ds(nx + 1 if side == XLO else 0, 1)]
        if pair:
            device["tm"] = partner
        return pltpu.make_async_remote_copy(
            src_ref=src, dst_ref=dst, send_sem=send_sem.at[to, side],
            recv_sem=recv_sem.at[to, side], device_id=device, device_id_type=MESH)

    def send_faces(i, sides, pair=False):
        for side in sides:
            @pl.when(has[side])
            def _(side=side):
                face_copy(i, side).start()
                if pair:
                    face_copy(i, side, True).start()

    def wait_faces(i, pair=False):
        for side in (YLO, YHI, XLO, XHI):
            @pl.when(has[side ^ 1])
            def _(side=side):
                face_copy(i, side, pair).wait_recv()

    half = nx // 2
    halves = (pl.ds(0, half), pl.ds(half, nx - half))

    def last_copy(i, part):
        field = fields[lasts[i]]
        if i == P_INIT:
            src = in_hbm.at[steps - 1, halves[part]]
        else:
            src = field.at[field.shape[0] - 1, (pl.ds(1, half), pl.ds(1 + half, nx - half))[part]]
        return pltpu.make_async_remote_copy(
            src_ref=src, dst_ref=before.at[i, halves[part]],
            send_sem=tsend.at[i, part], recv_sem=trecv.at[i, part],
            device_id={"tm": tm + 1}, device_id_type=MESH)

    lasts = (INIT, FIRST, ERR1, ERR2, FIX1, SUM0, SOL)

    def send_last(i, part):
        @pl.when(tm < n_tm - 1)
        def _():
            last_copy(i, part).start()

    def wait_last(i, parts=(0, 1)):
        @pl.when(tm > 0)
        def _():
            for part in parts:
                last_copy(i, part).wait_recv()

    send_faces(KAPPA, (XLO, XHI))
    send_faces(INIT, (XLO, XHI))
    send_last(P_INIT, 0)
    send_last(P_INIT, 1)

    def over_rows(body, by=8, start=0, stop=nx):
        def step(x, carry):
            body(x)
            return carry

        lax.fori_loop(start, stop, step, 0, unroll=by)

    def phase(body, i, send_part=None, pair=False, awaited=None):
        if awaited is not None:
            wait_last(awaited, (0,))
        body(0)
        if awaited is None:
            body(nx - 1)
            send_faces(i, (XLO, XHI), pair)
        else:
            send_faces(i, (XLO,), pair)
        over_rows(body, half - 1, 1, half)
        if send_part is not None:
            send_part(0)
        if awaited is not None:
            wait_last(awaited, (1,))
            body(nx - 1)
            send_faces(i, (XHI,), pair)
        over_rows(body, half - 1, half, nx - 1)
        send_faces(i, (YLO, YHI), pair)
        if send_part is not None:
            send_part(1)

    def put_faces(i, t, x, value):
        ysend[i][0, t, pl.ds(x, 1), :] = value[0:1, :]
        ysend[i][1, t, pl.ds(x, 1), :] = value[ny - 1:ny, :]

    def put(i, t, x, value):
        fields[i][t, x + 1] = value
        put_faces(i, t, x, value)

    loads[0].wait()
    loads[1].wait()

    def pack(x):
        put_faces(KAPPA, 0, x, fields[KAPPA][0, x + 1])
        for t in range(steps):
            put_faces(INIT, t, x, fields[INIT][t, x + 1])

    over_rows(pack)
    send_faces(KAPPA, (YLO, YHI))
    send_faces(INIT, (YLO, YHI))

    @pl.when(sx == 0)
    def _():
        for i in range(FIELDS):
            for t in range(fields[i].shape[0]):
                fields[i][t, 0] = jnp.zeros((ny, nz), jnp.float32)

    @pl.when(sx == n_sx - 1)
    def _():
        for i in range(FIELDS):
            for t in range(fields[i].shape[0]):
                fields[i][t, nx + 1] = jnp.zeros((ny, nz), jnp.float32)

    @pl.when(sy == 0)
    def _():
        for i in range(FIELDS):
            yrecv[i][0] = jnp.zeros(yrecv[i].shape[1:], jnp.float32)

    @pl.when(sy == n_sy - 1)
    def _():
        for i in range(FIELDS):
            yrecv[i][1] = jnp.zeros(yrecv[i].shape[1:], jnp.float32)

    @pl.when(tm == 0)
    def _():
        def clear(x):
            for i in range(7):
                before[i, x] = jnp.zeros((ny, nz), jnp.float32)

        over_rows(clear, 1)

    row = lax.broadcasted_iota(jnp.int32, (ny, nz), 0)
    column = lax.broadcasted_iota(jnp.int32, (ny, nz), 1)

    def around(i, t, x):
        field = fields[i]
        here = field[t, x + 1]
        return here, (
            field[t, x + 2],
            field[t, x],
            jnp.where(row == ny - 1, yrecv[i][1, t, pl.ds(x, 1), :], pltpu.roll(here, ny - 1, 0)),
            jnp.where(row == 0, yrecv[i][0, t, pl.ds(x, 1), :], pltpu.roll(here, 1, 0)),
            pltpu.roll(here, nz - 1, 1),
            pltpu.roll(here, 1, 1),
        )

    def beside(i, t, x, g):
        here, sides = around(i, t, x)
        terms = [g[j] * sides[j] for j in range(6)]
        return here, (terms[0] + terms[1]) + (terms[2] + terms[3]) + (terms[4] + terms[5])

    def faces_at(x):
        return [face[j, x] for j in range(6)]

    wait_faces(KAPPA)

    def coefficients(x):
        here, sides = around(KAPPA, 0, x)
        sides = list(sides)
        sides[4] = jnp.where(column == nz - 1, 0.0, sides[4])
        sides[5] = jnp.where(column == 0, 0.0, sides[5])
        g = [0.5 * (here + side) for side in sides]
        total = (g[0] + g[1]) + (g[2] + g[3]) + (g[4] + g[5])
        coupling[x] = total
        g[4] = jnp.where(column == nz - 1, 0.0, g[4])
        g[5] = jnp.where(column == 0, 0.0, g[5])
        for j in range(6):
            face[j, x] = g[j]
        for level in range(4):
            factor[level, x] = relax_weight / (1.0 + (2.0 ** level) * total)

    over_rows(coefficients)
    loads[2].wait()
    wait_faces(INIT)

    def sweep_first(x):
        g, f = faces_at(x), factor[0, x]
        running = before[P_INIT, x]
        for t in range(steps):
            here, near = beside(INIT, t, x, g)
            running = keep_weight * here + f * (hs[t, x] + near + running)
            put(FIRST, t, x, running)

    phase(sweep_first, FIRST, functools.partial(send_last, P_FIRST), awaited=P_INIT)
    wait_faces(FIRST)

    def down_one(x):
        g, diagonal, f = faces_at(x), 1.0 + coupling[x], factor[1, x]
        earlier = before[P_FIRST, x]
        running = None
        for m in range(steps // 2):
            total = None
            for t in (2 * m, 2 * m + 1):
                here, near = beside(FIRST, t, x, g)
                value = hs[t, x] + earlier - (diagonal * here - near)
                total = value if total is None else total + value
                earlier = here
            rhs1[m, x] = total
            running = f * total if running is None else f * (total + running)
            put(ERR1, m, x, running)

    phase(down_one, ERR1, functools.partial(send_last, P_ERR1), awaited=P_FIRST)
    wait_faces(ERR1)
    wait_last(P_ERR1)

    def down_two(x):
        g, diagonal, f = faces_at(x), 1.0 + 2.0 * coupling[x], factor[2, x]
        earlier = before[P_ERR1, x]
        total = None
        for t in range(2):
            here, near = beside(ERR1, t, x, g)
            value = rhs1[t, x] + earlier - (diagonal * here - 2.0 * near)
            total = value if total is None else total + value
            earlier = here
        rhs2[x] = total
        put(ERR2, 0, x, f * total)

    phase(down_two, ERR2, functools.partial(send_last, P_ERR2))
    wait_faces(ERR2)
    if n_tm > 2:
        wait_last(P_ERR2)

    def down_three(x):
        g, diagonal = faces_at(x), 1.0 + 4.0 * coupling[x]
        here, near = beside(ERR2, 0, x, g)
        earlier = here + before[P_ERR2, x] if n_tm > 2 else here
        value = rhs2[x] + jnp.where(even, earlier, 0.0) - (diagonal * here - 4.0 * near)
        mine[x] = value
        if n_tm == 2:
            put(PART, 0, x, factor[3, x] * value)

    def swap(part):
        return pltpu.make_async_remote_copy(
            src_ref=mine.at[halves[part]], dst_ref=theirs.at[halves[part]],
            send_sem=qsend.at[part], recv_sem=qrecv.at[part],
            device_id={"tm": partner}, device_id_type=MESH)

    if n_tm == 2:
        phase(down_three, PART, lambda part: swap(part).start(), True)
        wait_faces(PART)

        def part_two(x):
            here, near = beside(PART, 0, x, faces_at(x))
            put(PART2, 0, x, keep_weight * here + factor[3, x] * (mine[x] + 8.0 * near))

        phase(part_two, PART2, None, True)
    else:
        over_rows(down_three)
        swap(0).start()
        swap(1).start()
    swap(0).wait_recv()
    swap(1).wait_recv()

    def chain_copy(i, field):
        src = field.at[0, pl.ds(1, nx)] if i == 0 else second
        return pltpu.make_async_remote_copy(
            src_ref=src, dst_ref=chain.at[i], send_sem=csend.at[i],
            recv_sem=crecv.at[i], device_id={"tm": tm + 2}, device_id_type=MESH)

    def chain_wait(i):
        if n_tm > 2:
            @pl.when(tm > 1)
            def _():
                chain_copy(i, fields[ERR3]).wait_recv()

            @pl.when(tm < 2)
            def _():
                def clear(x):
                    chain[i, x] = jnp.zeros((ny, nz), jnp.float32)

                over_rows(clear, 1)

    def chain_send(i):
        if n_tm > 2:
            @pl.when(tm < n_tm - 2)
            def _():
                chain_copy(i, fields[ERR3]).start()

    chain_wait(0)

    def coarse_one(x):
        total = mine[x] + theirs[x]
        rhs3[x] = total
        if n_tm > 2:
            total = total + chain[0, x]
        value = factor[3, x] * total
        if n_tm > 2:
            put(ERR3, 0, x, value)
        else:
            fields[ERR3][0, x + 1] = value

    if n_tm > 2:
        phase(coarse_one, ERR3)
        chain_send(0)
        wait_faces(ERR3)
    else:
        over_rows(coarse_one)
        wait_faces(PART, True)
        for edge in (0, nx + 1):
            fields[ERR3][0, edge] = fields[PART][0, edge] + fields[PAIR][0, edge]
        for edge in range(2):
            yrecv[ERR3][edge, 0] = yrecv[PART][edge, 0] + yrecv[PAIR][edge, 0]
    if n_tm == 2:
        wait_last(P_ERR2)
    chain_wait(1)

    def coarse_two(x):
        here, near = beside(ERR3, 0, x, faces_at(x))
        total = rhs3[x] + 8.0 * near
        if n_tm > 2:
            total = total + chain[1, x]
        value = keep_weight * here + factor[3, x] * total
        if n_tm > 2:
            second[x] = value
            earlier = jnp.where(even, chain[1, x], value)
        else:
            earlier = jnp.where(even, 0.0, value)
        mine_next[x] = before[P_ERR2, x] + earlier
        value = fields[ERR2][0, x + 1] + value
        if n_tm > 2:
            put(FIX2, 0, x, value)
        else:
            fields[FIX2][0, x + 1] = value

    mine_next = res.at[0]
    if n_tm > 2:
        phase(coarse_two, FIX2)
        chain_send(1)
        wait_faces(FIX2)
    else:
        over_rows(coarse_two)
        wait_faces(PART2)
        wait_faces(PART2, True)
        for edge in (0, nx + 1):
            fields[FIX2][0, edge] = fields[ERR2][0, edge] + (
                fields[PART2][0, edge] + fields[PAIR2][0, edge])
        for edge in range(2):
            yrecv[FIX2][edge, 0] = yrecv[ERR2][edge, 0] + (
                yrecv[PART2][edge, 0] + yrecv[PAIR2][edge, 0])

    def up_two(x):
        here, near = beside(FIX2, 0, x, faces_at(x))
        value = keep_weight * here + factor[2, x] * (rhs2[x] + 4.0 * near + mine_next[x])
        for m in range(2):
            put(FIX1, m, x, fields[ERR1][m, x + 1] + value)

    phase(up_two, FIX1, functools.partial(send_last, P_FIX1))
    wait_faces(FIX1)

    def up_one(x):
        g, f = faces_at(x), factor[1, x]
        running = before[P_FIX1, x]
        for m in range(2):
            here, near = beside(FIX1, m, x, g)
            running = keep_weight * here + f * (rhs1[m, x] + 2.0 * near + running)
            for t in (2 * m, 2 * m + 1):
                put(SUM0, t, x, fields[FIRST][t, x + 1] + running)

    phase(up_one, SUM0, functools.partial(send_last, P_SUM0), awaited=P_FIX1)
    wait_faces(SUM0)
    wait_last(P_SUM0)

    def up_zero(x):
        g, f = faces_at(x), factor[0, x]
        running = before[P_SUM0, x]
        for t in range(steps):
            here, near = beside(SUM0, t, x, g)
            running = keep_weight * here + f * (hs[t, x] + near + running)
            put(SOL, t, x, running)

    phase(up_zero, SOL, functools.partial(send_last, P_SOL))
    out_one = pltpu.make_async_copy(fields[SOL].at[:, pl.ds(1, nx)], sol_hbm, local.at[3])
    out_one.start()
    wait_faces(SOL)
    wait_last(P_SOL)

    def last_defect(x):
        g, diagonal = faces_at(x), 1.0 + coupling[x]
        earlier = before[P_SOL, x]
        for t in range(steps):
            here, near = beside(SOL, t, x, g)
            res[t, x] = hs[t, x] + earlier - (diagonal * here - near)
            earlier = here

    over_rows(last_defect)
    out_two = pltpu.make_async_copy(res, res_hbm, local.at[4])
    out_two.start()

    for i in range(FIELDS):
        if i in ((PAIR, PAIR2, ERR3, FIX2) if n_tm == 2 else (PART, PAIR, PART2, PAIR2)):
            continue
        for side in (XLO, XHI, YLO, YHI):
            @pl.when(has[side])
            def _(i=i, side=side):
                face_copy(i, side).wait_send()
                if i in (PART, PART2):
                    face_copy(i, side, True).wait_send()

    @pl.when(tm < n_tm - 1)
    def _():
        for i in range(7):
            for part in range(2):
                last_copy(i, part).wait_send()

    swap(0).wait_send()
    swap(1).wait_send()
    if n_tm > 2:
        @pl.when(tm < n_tm - 2)
        def _():
            for i in range(2):
                chain_copy(i, fields[ERR3]).wait_send()

    out_one.wait()
    out_two.wait()


def solution(mesh):
    n_tm, n_sx, n_sy = (mesh.shape[axis] for axis in ("tm", "sx", "sy"))
    f32 = jnp.float32

    def per_device(heat_source, conductivity, initial_iterate):
        steps, nx, ny, nz = heat_source.shape
        depth = (1, steps, steps, steps // 2, 1, 1, 1, steps // 2, steps, steps, 1, 1, 1, 1)
        scratch = [pltpu.VMEM((d, nx + 2, ny, nz), f32) for d in depth]
        scratch += [pltpu.VMEM((2, d, nx, nz), f32) for d in depth] * 2
        cells = (nx, ny, nz)
        dma = pltpu.SemaphoreType.DMA
        scratch += [
            pltpu.VMEM((steps,) + cells, f32),
            pltpu.VMEM((steps,) + cells, f32),
            pltpu.VMEM((7,) + cells, f32),
            pltpu.VMEM(cells, f32),
            pltpu.VMEM((steps // 2,) + cells, f32),
            pltpu.VMEM(cells, f32),
            pltpu.VMEM(cells, f32),
            pltpu.VMEM(cells, f32),
            pltpu.VMEM(cells, f32),
            pltpu.VMEM((2,) + cells, f32),
            pltpu.VMEM((6,) + cells, f32),
            pltpu.VMEM(cells, f32),
            pltpu.VMEM((4,) + cells, f32),
            dma((FIELDS, 4)), dma((FIELDS, 4)), dma((7, 2)), dma((7, 2)),
            dma((2,)), dma((2,)), dma((2,)), dma((2,)), dma((5,)),
        ]
        field = jax.ShapeDtypeStruct(heat_source.shape, f32)
        return pl.pallas_call(
            functools.partial(kernel, n_tm, n_sx, n_sy),
            out_shape=(field, field),
            in_specs=[pl.BlockSpec(memory_space=pltpu.HBM)] * 3,
            out_specs=(pl.BlockSpec(memory_space=pltpu.HBM),) * 2,
            scratch_shapes=scratch,
            compiler_params=pltpu.CompilerParams(
                collective_id=0, has_side_effects=True, vmem_limit_bytes=67043328
            ),
            name="vcycle",
        )(heat_source, conductivity, initial_iterate)

    placed = (P("tm", "sx", "sy", None), P("sx", "sy", None), P("tm", "sx", "sy", None))
    return jax.shard_map(
        per_device,
        mesh=mesh,
        in_specs=placed,
        out_specs=(P("tm", "sx", "sy", None), P("tm", "sx", "sy", None)),
        check_vma=False,
    )
```

profile of v0, /device:TPU:3, one launch (start us, length us, event | category | flops | bytes accessed | tf_op | source)
XLA Modules:
  0.0 41.2 jit_solution(9203452207875799012)
XLA Ops:
  0.6 37.8 %vcycle.1 = (f32[4,16,16,128]{3,2,1,0:T(8,128)}, f32[4,16,16,128]{3,2,1,0:T(8,128)}) custom-call(f32[4,16,16,128]{3,2,1,0:T(8,128)} %hs_hbm.1, f32[16,16,128]{2,1,0:T(8,128)} %k_hbm.1, f32[4,16,16,128]{3,2,1,0:T(8,128)} %in_hbm.1), custom_call_target="tpu_custom_call" | custom-call | tf_op jit(solution)/shard_map/vcycle/pallas_call | solution.py:534
  38.5 0.0 copy-start
  38.5 1.9 %copy.7 = f32[4,16,16,128]{3,2,1,0:T(8,128)} copy(f32[4,16,16,128]{3,2,1,0:T(8,128)} %get-tuple-element.4) | data formatting | bytes 1048576
  40.4 0.0 copy-done
  40.4 0.8 %copy.8 = f32[4,16,16,128]{3,2,1,0:T(8,128)} copy(f32[4,16,16,128]{3,2,1,0:T(8,128)S(1)} %copy-done) | data formatting | bytes 1048576
Async XLA Ops:
  38.5 1.9 %copy-start = (f32[4,16,16,128]{3,2,1,0:T(8,128)S(1)}, f32[4,16,16,128]{3,2,1,0:T(8,128)}, u32[]{:S(2)}) copy-start(f32[4,16,16,128]{3,2,1,0:T(8,128)} %get-tuple-element.5) | copy-start | bytes 1572868
where the time goes:
time: 41.4 us; the launch traced here: 41.2 us
  Pallas kernels  37.8 us (91%)
  local copies, waits for them, and re-layouts  2.72 us (7%)
  between operations  0.65 us (2%)
    pallas_call x1, Pallas kernels, per_device(): pl.pallas_call(functools.partial(kernel, n_tm, n_sx, n_sy), out_shape=(fi...  37.8 us
    unnamed x4, local copies, waits for them, and re-layouts  2.72 us

commit v1 on v0

--- a/solution.py
+++ b/solution.py
@@ -455,10 +455,9 @@
             here, near = beside(SUM0, t, x, g)
             running = keep_weight * here + f * (hs[t, x] + near + running)
             put(SOL, t, x, running)
+            sol_hbm[t, x] = running
 
     phase(up_zero, SOL, functools.partial(send_last, P_SOL))
-    out_one = pltpu.make_async_copy(fields[SOL].at[:, pl.ds(1, nx)], sol_hbm, local.at[3])
-    out_one.start()
     wait_faces(SOL)
     wait_last(P_SOL)
 
@@ -467,12 +466,10 @@
         earlier = before[P_SOL, x]
         for t in range(steps):
             here, near = beside(SOL, t, x, g)
-            res[t, x] = hs[t, x] + earlier - (diagonal * here - near)
+            res_hbm[t, x] = hs[t, x] + earlier - (diagonal * here - near)
             earlier = here
 
     over_rows(last_defect)
-    out_two = pltpu.make_async_copy(res, res_hbm, local.at[4])
-    out_two.start()
 
     for i in range(FIELDS):
         if i in ((PAIR, PAIR2, ERR3, FIX2) if n_tm == 2 else (PART, PAIR, PART2, PAIR2)):
@@ -498,8 +495,13 @@
             for i in range(2):
                 chain_copy(i, fields[ERR3]).wait_send()
 
-    out_one.wait()
-    out_two.wait()
+
+def store(one, two, one_hbm, two_hbm, sem):
+    copies = [pltpu.make_async_copy(one, one_hbm, sem.at[0]), pltpu.make_async_copy(two, two_hbm, sem.at[1])]
+    for copy in copies:
+        copy.start()
+    for copy in copies:
+        copy.wait()
 
 
 def solution(mesh):
@@ -531,17 +533,25 @@
             dma((2,)), dma((2,)), dma((2,)), dma((2,)), dma((5,)),
         ]
         field = jax.ShapeDtypeStruct(heat_source.shape, f32)
-        return pl.pallas_call(
+        one, two = pl.pallas_call(
             functools.partial(kernel, n_tm, n_sx, n_sy),
-            out_shape=(field, field),
+            out_shape=(pltpu.VMEM(heat_source.shape, f32),) * 2,
             in_specs=[pl.BlockSpec(memory_space=pltpu.HBM)] * 3,
-            out_specs=(pl.BlockSpec(memory_space=pltpu.HBM),) * 2,
+            out_specs=(pl.BlockSpec(memory_space=pltpu.VMEM),) * 2,
             scratch_shapes=scratch,
             compiler_params=pltpu.CompilerParams(
-                collective_id=0, has_side_effects=True, vmem_limit_bytes=67043328
+                collective_id=0, has_side_effects=True, vmem_limit_bytes=40000000
             ),
             name="vcycle",
-        )(heat_source, conductivity, initial_iterate)
+        )(*(pltpu.with_memory_space_constraint(x, pltpu.HBM) for x in (heat_source, conductivity, initial_iterate)))
+        return pl.pallas_call(
+            store,
+            out_shape=(field, field),
+            in_specs=[pl.BlockSpec(memory_space=pltpu.VMEM)] * 2,
+            out_specs=(pl.BlockSpec(memory_space=pltpu.HBM),) * 2,
+            scratch_shapes=[dma((2,))],
+            name="store",
+        )(*(pltpu.with_memory_space_constraint(x, pltpu.VMEM) for x in (one, two)))
 
     placed = (P("tm", "sx", "sy", None), P("sx", "sy", None), P("tm", "sx", "sy", None))
     return jax.shard_map(

time: 41.4 us -> 38.9 us (0.940)
  local copies, waits for them, and re-layouts: 2.72 us -> 0 us
    unnamed x4 -> x0, local copies, waits for them, and re-layouts: 2.72 us -> none
    pallas_call x1 -> x2, Pallas kernels: 37.8 us -> 38.1 us  [the longest x1 37.1 us: per_device(): pl.pallas_call(functools.partial(kernel, n_tm, n_sx, n_sy), out_shape=(pl...]
where the time goes in v1:
time: 38.9 us; the launch traced here: 38.7 us
  Pallas kernels  38.1 us (98%)
  between operations  0.64 us (2%)
    pallas_call x1, Pallas kernels, per_device(): pl.pallas_call(functools.partial(kernel, n_tm, n_sx, n_sy), out_shape=(pl...  37.1 us
    pallas_call x1, Pallas kernels, per_device(): pl.pallas_call(store, out_shape=(field, field), in_specs=[pl.BlockSpec(me...  0.99 us

profile of v1, /device:TPU:3, one launch (start us, length us, event | category | flops | bytes accessed | tf_op | source)
XLA Modules:
  0.0 38.7 jit_solution(8037144744497400071)
XLA Ops:
  0.6 37.1 %vcycle.1 = (f32[4,16,16,128]{3,2,1,0:T(8,128)S(1)}, f32[4,16,16,128]{3,2,1,0:T(8,128)S(1)}) custom-call(f32[4,16,16,128]{3,2,1,0:T(8,128)} %hs_hbm.1, f32[16,16,128]{2,1,0:T(8,128)} %k_hbm.1, f32[4,16,16,128]{3,2,1,0:T(8,128)} %in_hbm.1), custom_call_target="tpu_custom_call" | custom-call | tf_op jit(solution)/shard_map/vcycle/pallas_call | solution.py:536
  37.8 1.0 %store.1 = (f32[4,16,16,128]{3,2,1,0:T(8,128)}, f32[4,16,16,128]{3,2,1,0:T(8,128)}) custom-call(f32[4,16,16,128]{3,2,1,0:T(8,128)S(1)} %get-tuple-element.4.one, f32[4,16,16,128]{3,2,1,0:T(8,128)S(1)} %get-tuple-element.5.two), custom_call_target="tpu_custom_call" | custom-call | tf_op jit(solution)/shard_map/store/pallas_call | solution.py:547

commit v2 on v1

--- a/solution.py
+++ b/solution.py
@@ -496,6 +496,563 @@
                 chain_copy(i, fields[ERR3]).wait_send()
 
 
+DEPTH = 6
+EDGE = 8
+EXCHANGES = {
+    "kappa": ("k", (0, 1), ()),
+    "kappa_far": ("k", (1, 6), ((0, 5, 0, 5),)),
+    "init": ("in", (0, 1), ()),
+    "source": ("hs", (0, 1), ()),
+    "first": ("first", (0, 1), ()),
+    "first_far": ("first", (1, 2), ((0, 1, 0, 1),)),
+    "pair": ("pair", (0, 2), ((0, 1, 0, 1),)),
+    "err": ("err", (0, 5), ((0, 4, 0, 4),)),
+    "last": ("last", (0, 5), ((0, 4, 0, 4),)),
+    "prev_one": ("prev", (0, 5), ((0, 4, 0, 4),)),
+    "prev_zero": ("prev", (0, 5), ((0, 4, 0, 4),)),
+    "rhs3": ("rhs3", (0, 5), ((0, 4, 0, 4),)),
+}
+NAMES = tuple(EXCHANGES)
+X_FACES = ((-1, 0), (1, 0))
+REST = ((0, -1), (0, 1), (-1, -1), (-1, 1), (1, -1), (1, 1))
+ALL = X_FACES + REST
+T_INIT, T_LAST, T_ONE, T_ZERO, T_MINE, T_GUESS = range(6)
+
+
+def wide_kernel(n_sx, n_sy, hs_hbm, k_hbm, in_hbm, sol_out, res_out,
+                kap, ini, src, first, pair, err, last, prev, sums, fr, rhs3, one, err3, wave,
+                err2, fix, vee, total, sol, face, coupling, factor,
+                before, mine, theirs, guess, ahead,
+                send_sem, recv_sem, tsend, trecv, local):
+    nx, ny, nz = k_hbm.shape
+    steps = in_hbm.shape[0]
+    wide = ny + 2 * EDGE
+    tm, sx, sy = lax.axis_index("tm"), lax.axis_index("sx"), lax.axis_index("sy")
+    at_one = jnp.where(tm > 0, 1.0, 0.0)
+    at_zero = 1.0 - at_one
+    mid = pl.ds(EDGE, ny)
+    inner = pl.ds(DEPTH, nx)
+    homes = {"k": kap, "in": ini, "hs": src, "first": first, "pair": pair, "err": err,
+             "last": last, "prev": prev, "rhs3": rhs3}
+    outside = {"k": k_hbm, "in": in_hbm, "hs": hs_hbm}
+
+    loads = [
+        pltpu.make_async_copy(k_hbm, kap.at[0, inner, mid], local.at[0]),
+        pltpu.make_async_copy(in_hbm, ini.at[:, inner, mid], local.at[1]),
+        pltpu.make_async_copy(hs_hbm, src.at[:, inner, mid], local.at[2]),
+    ]
+    for load in loads:
+        load.start()
+
+    def there(way, sign=1):
+        ok = None
+        for step, at, size in ((sign * way[0], sx, n_sx), (sign * way[1], sy, n_sy)):
+            if step:
+                here = at > 0 if step < 0 else at < size - 1
+                ok = here if ok is None else jnp.logical_and(ok, here)
+        return ok
+
+    def target(way):
+        device = {}
+        if way[0]:
+            device["sx"] = sx + way[0]
+        if way[1]:
+            device["sy"] = sy + way[1]
+        return device
+
+    barrier = pltpu.get_barrier_semaphore()
+    count = jnp.int32(1)
+    for way in ALL:
+        count = count + jnp.where(there(way), 1, 0)
+
+        @pl.when(there(way))
+        def _(way=way):
+            pl.semaphore_signal(barrier, inc=1, device_id=target(way), device_id_type=MESH)
+
+    pl.semaphore_signal(barrier, inc=1, device_id={"tm": 1 - tm}, device_id_type=MESH)
+
+    def rows(body, depth, by=4):
+        def step(x, carry):
+            body(x)
+            return carry
+
+        lax.fori_loop(DEPTH - depth, DEPTH + nx + depth, step, 0, unroll=by)
+
+    filled = ((kap, 6), (ini, 1), (src, 1), (first, 2), (pair, 2), (err, 5), (last, 5), (prev, 5), (rhs3, 5))
+    plane = jnp.zeros((wide, nz), jnp.float32)
+    strip = jnp.zeros((EDGE, nz), jnp.float32)
+
+    def fill(edge_rows):
+        for array, depth in filled:
+            for t in range(array.shape[0]):
+                for i in range(depth):
+                    array[t, DEPTH - 1 - i if edge_rows < 0 else DEPTH + nx + i] = plane
+
+    def fill_side(start):
+        for array, depth in filled:
+            def body(x):
+                for t in range(array.shape[0]):
+                    array[t, x, pl.ds(start, EDGE), :] = strip
+
+            rows(body, depth)
+
+    @pl.when(sx == 0)
+    def _():
+        fill(-1)
+
+    @pl.when(sx == n_sx - 1)
+    def _():
+        fill(1)
+
+    @pl.when(sy == 0)
+    def _():
+        fill_side(0)
+
+    @pl.when(sy == n_sy - 1)
+    def _():
+        fill_side(EDGE + ny)
+
+    @pl.when(tm == 0)
+    def _():
+        def body(x):
+            last[0, x] = plane
+            prev[0, x] = plane
+            prev[1, x] = plane
+
+        rows(body, 5)
+
+        def empty(x):
+            before[x - DEPTH] = jnp.zeros((ny, nz), jnp.float32)
+            ahead[x - DEPTH] = jnp.zeros((ny, nz), jnp.float32)
+
+        rows(empty, 0)
+
+    pl.semaphore_wait(barrier, count)
+
+    def span(step, size, low, high):
+        if step == 0:
+            return 0, size, 0
+        if step < 0:
+            return low, high - low, size + low
+        return size - high, high - low, -high
+
+    def pieces(name, ways):
+        kind, (low, high), corners = EXCHANGES[name]
+        slot = 0
+        for way in ALL:
+            boxes = corners if way[0] and way[1] else ((low, high, low, high),)
+            for box in boxes:
+                if way in ways:
+                    yield way, box, slot
+                slot += 1
+
+    def copy_of(name, way, box, slot):
+        kind = EXCHANGES[name][0]
+        land = homes[kind]
+        fx, wx, tx = span(way[0], nx, box[0], box[1])
+        fy, wy, ty = span(way[1], ny, box[2], box[3])
+        steps_at = {"prev_zero": pl.ds(0, 1), "prev_one": pl.ds(1, 1)}.get(name, slice(None))
+        if kind == "k":
+            source = k_hbm.at[pl.ds(fx, wx), pl.ds(fy, wy)]
+            dest = land.at[0, pl.ds(DEPTH + tx, wx), pl.ds(EDGE + ty, wy)]
+        else:
+            if kind in outside:
+                source = outside[kind].at[:, pl.ds(fx, wx), pl.ds(fy, wy)]
+            else:
+                source = land.at[steps_at, pl.ds(DEPTH + fx, wx), pl.ds(EDGE + fy, wy)]
+            dest = land.at[steps_at, pl.ds(DEPTH + tx, wx), pl.ds(EDGE + ty, wy)]
+        number = NAMES.index(name)
+        return pltpu.make_async_remote_copy(
+            src_ref=source, dst_ref=dest, send_sem=send_sem.at[number, slot],
+            recv_sem=recv_sem.at[number, slot], device_id=target(way), device_id_type=MESH)
+
+    def send(name, ways=ALL):
+        for way, box, slot in pieces(name, ways):
+            @pl.when(there(way))
+            def _(way=way, box=box, slot=slot):
+                copy_of(name, way, box, slot).start()
+
+    def wait(name):
+        for way, box, slot in pieces(name, REST + X_FACES):
+            @pl.when(there(way, -1))
+            def _(way=way, box=box, slot=slot):
+                copy_of(name, way, box, slot).wait_recv()
+
+    def wait_sent(name):
+        for way, box, slot in pieces(name, ALL):
+            @pl.when(there(way))
+            def _(way=way, box=box, slot=slot):
+                copy_of(name, way, box, slot).wait_send()
+
+    half = nx // 2
+    ends = ((0, half), (half, nx - half))
+
+    def across(which, part):
+        low, size = ends[part]
+        near, far = pl.ds(low, size), pl.ds(DEPTH + low, size)
+        source, dest = {
+            T_INIT: lambda: (in_hbm.at[steps - 1, near], before.at[near]),
+            T_LAST: lambda: (first.at[steps - 1, far, mid], last.at[0, far, mid]),
+            T_ONE: lambda: (err.at[1, far, mid], prev.at[1, far, mid]),
+            T_ZERO: lambda: (err.at[0, far, mid], prev.at[0, far, mid]),
+            T_MINE: lambda: (mine.at[near], theirs.at[near]),
+            T_GUESS: lambda: (guess.at[near], ahead.at[near]),
+        }[which]()
+        return pltpu.make_async_remote_copy(
+            src_ref=source, dst_ref=dest, send_sem=tsend.at[which, part],
+            recv_sem=trecv.at[which, part], device_id={"tm": 1 - tm}, device_id_type=MESH)
+
+    def pass_on(which, parts=(0, 1)):
+        @pl.when(tm == 0)
+        def _():
+            for part in parts:
+                across(which, part).start()
+
+    def arrive(which, parts=(0, 1)):
+        @pl.when(tm > 0)
+        def _():
+            for part in parts:
+                across(which, part).wait_recv()
+
+    send("kappa")
+    send("init")
+    pass_on(T_INIT)
+    send("source")
+    send("kappa_far")
+
+    column = lax.broadcasted_iota(jnp.int32, (wide, nz), 1)
+    height = lax.broadcasted_iota(jnp.int32, (wide, nz), 0)
+    low_side = jnp.where(sy == 0, EDGE, 0)
+    high_side = jnp.where(sy == n_sy - 1, EDGE + ny, wide)
+    within = jnp.logical_and(height >= low_side, height < high_side)
+    low_row = jnp.where(sx == 0, DEPTH, 0)
+    high_row = jnp.where(sx == n_sx - 1, DEPTH + nx, nx + 2 * DEPTH)
+
+    def around(ref, t, x):
+        here = ref[t, x]
+        return here, (
+            ref[t, x + 1], ref[t, x - 1],
+            pltpu.roll(here, wide - 1, 0), pltpu.roll(here, 1, 0),
+            pltpu.roll(here, nz - 1, 1), pltpu.roll(here, 1, 1),
+        )
+
+    def around_mid(ref, t, x):
+        here = ref[t, x, mid, :]
+        return here, (
+            ref[t, x + 1, mid, :], ref[t, x - 1, mid, :],
+            ref[t, x, pl.ds(EDGE + 1, ny), :], ref[t, x, pl.ds(EDGE - 1, ny), :],
+            pltpu.roll(here, nz - 1, 1), pltpu.roll(here, 1, 1),
+        )
+
+    def beside(ref, t, x, g):
+        here, sides = (around if g[0].shape[0] == wide else around_mid)(ref, t, x)
+        terms = [g[j] * sides[j] for j in range(6)]
+        return here, (terms[0] + terms[1]) + (terms[2] + terms[3]) + (terms[4] + terms[5])
+
+    def faces(x):
+        return [face[j, x] for j in range(6)]
+
+    def faces_mid(x):
+        return [face[j, x, mid, :] for j in range(6)]
+
+    def couple(here, sides, col):
+        sides = list(sides)
+        top, bottom = col == nz - 1, col == 0
+        sides[4] = jnp.where(top, 0.0, sides[4])
+        sides[5] = jnp.where(bottom, 0.0, sides[5])
+        g = [0.5 * (here + side) for side in sides]
+        whole = (g[0] + g[1]) + (g[2] + g[3]) + (g[4] + g[5])
+        g[4] = jnp.where(top, 0.0, g[4])
+        g[5] = jnp.where(bottom, 0.0, g[5])
+        return g, whole
+
+    def coefficients_mid(x):
+        g, whole = couple(*around_mid(kap, 0, x), column[:ny])
+        coupling[x, mid, :] = whole
+        for j in range(6):
+            face[j, x, mid, :] = g[j]
+        for level in range(2):
+            factor[level, x, mid, :] = relax_weight / (1.0 + (2.0 ** level) * whole)
+
+    def coefficients(x):
+        g, whole = couple(*around(kap, 0, x), column)
+        coupling[x] = whole
+        inside = jnp.logical_and(within, jnp.logical_and(x >= low_row, x < high_row))
+        for j in range(6):
+            face[j, x] = g[j]
+        for level in range(4):
+            factor[level, x] = jnp.where(inside, relax_weight / (1.0 + (2.0 ** level) * whole), 0.0)
+
+    def phase(body, edge, name):
+        for i in range(edge):
+            body(DEPTH + i)
+            body(DEPTH + nx - 1 - i)
+        send(name, X_FACES)
+
+        def step(x, carry):
+            body(x)
+            return carry
+
+        lax.fori_loop(DEPTH + edge, DEPTH + nx - edge, step, 0, unroll=4)
+        send(name, REST)
+
+    loads[0].wait()
+    wait("kappa")
+    rows(coefficients_mid, 0)
+    loads[1].wait()
+    loads[2].wait()
+    wait("init")
+    arrive(T_INIT)
+
+    def sweep_first(x):
+        g, f = faces_mid(x), factor[0, x, mid, :]
+        running = before[x - DEPTH]
+        for t in range(steps):
+            here, near = beside(ini, t, x, g)
+            running = keep_weight * here + f * (src[t, x, mid, :] + near + running)
+            first[t, x, mid, :] = running
+
+    phase(sweep_first, 1, "first")
+    pass_on(T_LAST)
+    wait("kappa_far")
+    rows(coefficients, 5)
+    send("first_far")
+    wait("first")
+
+    def down_one(x):
+        g, f, c = faces_mid(x), factor[0, x, mid, :], coupling[x, mid, :]
+        f_one = factor[1, x, mid, :]
+        diagonal = 1.0 + c
+        earlier = None
+        ahead_value = None
+        running = None
+        pair_zero = None
+        for m in range(2):
+            both = None
+            for t in (2 * m, 2 * m + 1):
+                here, near = beside(first, t, x, g)
+                supply = src[t, x, mid, :] + near
+                value = supply - diagonal * here
+                if earlier is not None:
+                    value = value + earlier
+                both = value if both is None else both + value
+                ahead_value = keep_weight * here + f * (supply if ahead_value is None else supply + ahead_value)
+                earlier = here
+            running = f_one * both if running is None else f_one * (both + running)
+            err[m, x, mid, :] = running
+            pair_zero = running if m == 0 else pair_zero
+        both = pair_zero + running
+        pair[1, x, mid, :] = both
+        pair[0, x, mid, :] = both + at_zero * ((f_one + f_one * f_one) * earlier)
+        pair[2, x, mid, :] = at_zero * running
+        guess[x - DEPTH] = ahead_value
+
+    phase(down_one, 2, "pair")
+    pass_on(T_ONE)
+    pass_on(T_ZERO)
+    send("err")
+    arrive(T_LAST)
+
+    @pl.when(tm > 0)
+    def _():
+        send("last")
+
+    wait("pair")
+
+    def down_two(x):
+        here, near = beside(pair, 0, x, faces(x))
+        value = 0.25 * (1.0 + 2.0 * coupling[x]) * here + 2.0 * near + pair[2, x]
+        fr[0, x] = factor[2, x] * value
+
+    rows(down_two, 1)
+
+    def down_three(x):
+        g, c = faces_mid(x), coupling[x, mid, :]
+        here, near = beside(fr, 0, x, g)
+        value = 0.25 * (1.0 + 4.0 * c) * here + 4.0 * near
+        here, near = beside(pair, 1, x, g)
+        base = factor[2, x, mid, :] * (0.25 * (1.0 + 2.0 * c) * here + 2.0 * near)
+        mine[x - DEPTH] = value + at_zero * base
+
+    rows(down_three, 0)
+    across(T_MINE, 0).start()
+    across(T_MINE, 1).start()
+    pass_on(T_GUESS)
+    arrive(T_ONE)
+
+    @pl.when(tm > 0)
+    def _():
+        send("prev_one")
+
+    arrive(T_ZERO)
+
+    @pl.when(tm > 0)
+    def _():
+        send("prev_zero")
+
+    across(T_MINE, 0).wait_recv()
+    across(T_MINE, 1).wait_recv()
+
+    def add_up(x):
+        rhs3[0, x, mid, :] = mine[x - DEPTH] + theirs[x - DEPTH]
+
+    rows(add_up, 0)
+    send("rhs3")
+
+    wait("err")
+    wait("first_far")
+
+    @pl.when(tm > 0)
+    def _():
+        wait("last")
+        wait("prev_one")
+        wait("prev_zero")
+
+    def gather_far(x):
+        f = factor[1, x]
+        sums[0, x] = err[0, x] + err[1, x] + (f + f * f) * last[0, x]
+        sums[1, x] = prev[0, x] + prev[1, x]
+
+    rows(gather_far, 5)
+
+    def level_two(x):
+        g, f, weight = faces(x), factor[2, x], 0.25 * (1.0 + 2.0 * coupling[x])
+        here, near = beside(sums, 0, x, g)
+        err2[0, x] = f * (weight * here + 2.0 * near + prev[1, x])
+        here, near = beside(sums, 1, x, g)
+        err2[1, x] = f * (weight * here + 2.0 * near)
+
+    rows(level_two, 4)
+
+    def own_errors(x):
+        f = factor[1, x]
+        carried = f * last[0, x]
+        return err[0, x] + carried, err[1, x] + f * carried
+
+    def fix_two(x):
+        g, f = faces(x), factor[2, x]
+        own, near = beside(err2, 0, x, g)
+        past, near_past = beside(err2, 1, x, g)
+        value = (2.0 - relax_weight) * own + f * (4.0 * near + past)
+        value_past = (2.0 - relax_weight) * past + 4.0 * (f * near_past)
+        zero, first_one = own_errors(x)
+        fix[0, x] = zero + value
+        fix[1, x] = first_one + value
+        fix[2, x] = prev[0, x] + value_past
+        fix[3, x] = prev[1, x] + value_past
+
+    rows(fix_two, 3)
+
+    def fix_one(x):
+        g, f = faces(x), factor[1, x]
+        here, near = [], []
+        for i in range(4):
+            a, b = beside(fix, i, x, g)
+            here.append(a)
+            near.append(keep_weight * a + 2.0 * (f * b))
+        zero, first_one = own_errors(x)
+        value = near[0] + zero + f * here[3]
+        vee[0, x] = value
+        vee[1, x] = near[1] + first_one + f * (value - zero)
+        value = near[2] + prev[0, x]
+        vee[2, x] = value
+        vee[3, x] = near[3] + prev[1, x] + f * (value - prev[0, x])
+
+    rows(fix_one, 2)
+    wait("rhs3")
+
+    def coarse_one(x):
+        one[0, x] = factor[3, x] * rhs3[0, x]
+
+    rows(coarse_one, 5)
+
+    def coarse_two(x):
+        here, near = beside(one, 0, x, faces(x))
+        err3[0, x] = keep_weight * here + factor[3, x] * (rhs3[0, x] + 8.0 * near)
+
+    rows(coarse_two, 4)
+
+    def up_two(x):
+        f = factor[2, x]
+        here, near = beside(err3, 0, x, faces(x))
+        value = keep_weight * here + 4.0 * (f * near)
+        wave[0, x] = value + at_one * (f * here)
+        wave[1, x] = value
+
+    rows(up_two, 3)
+
+    def up_one(x):
+        g, f = faces(x), factor[1, x]
+        here, near = beside(wave, 0, x, g)
+        past, near_past = beside(wave, 1, x, g)
+        own = keep_weight * here + 2.0 * (f * near)
+        shadow = at_one * (keep_weight * past + 2.0 * (f * near_past))
+        zero = own + at_one * (f * past)
+        gain = (vee[0, x] + zero, vee[1, x] + own + f * zero)
+        for t in range(steps):
+            total[t, x] = first[t, x] + gain[t // 2]
+        vee[2, x] = vee[2, x] + shadow
+        vee[3, x] = vee[3, x] + shadow + f * shadow
+
+    rows(up_one, 2)
+    wait("source")
+
+    def up_zero(x):
+        g, f = faces(x), factor[0, x]
+        running = last[0, x] + vee[3, x]
+        for t in range(steps):
+            here, near = beside(total, t, x, g)
+            running = keep_weight * here + f * (src[t, x] + near + running)
+            sol[t, x] = running
+
+    rows(up_zero, 1)
+    arrive(T_GUESS)
+
+    def finish(x):
+        g, f = faces_mid(x), factor[0, x, mid, :]
+        diagonal = 1.0 + coupling[x, mid, :]
+        lifted = []
+        for i in (2, 3):
+            here, near = beside(vee, i, x, g)
+            lifted.append(keep_weight * here + f * near)
+        earlier = ahead[x - DEPTH] + (1.0 + f) * (f * f * lifted[0] + lifted[1])
+        for t in range(steps):
+            here, near = beside(sol, t, x, g)
+            sol_out[t, x - DEPTH] = here
+            res_out[t, x - DEPTH] = src[t, x, mid, :] + earlier - (diagonal * here - near)
+            earlier = here
+
+    rows(finish, 0)
+
+    for name in NAMES:
+        if name in ("last", "prev_one", "prev_zero"):
+            @pl.when(tm > 0)
+            def _(name=name):
+                wait_sent(name)
+        else:
+            wait_sent(name)
+
+    @pl.when(tm == 0)
+    def _():
+        for which in (T_INIT, T_LAST, T_ONE, T_ZERO, T_GUESS):
+            for part in range(2):
+                across(which, part).wait_send()
+
+    across(T_MINE, 0).wait_send()
+    across(T_MINE, 1).wait_send()
+
+
+def wide_scratch(steps, nx, ny, nz):
+    f32, dma = jnp.float32, pltpu.SemaphoreType.DMA
+    depths = (1, steps, steps, steps, 3, 2, 1, 2, 2, 1, 1, 1, 1, 2, 2, 4, 4, steps, steps, 6)
+    large = (nx + 2 * DEPTH, ny + 2 * EDGE, nz)
+    scratch = [pltpu.VMEM((d,) + large, f32) for d in depths]
+    scratch += [pltpu.VMEM(large, f32), pltpu.VMEM((4,) + large, f32)]
+    scratch += [pltpu.VMEM((nx, ny, nz), f32)] * 5
+    scratch += [dma((len(NAMES), 12)), dma((len(NAMES), 12)), dma((6, 2)), dma((6, 2)), dma((3,))]
+    return scratch
+
+
 def store(one, two, one_hbm, two_hbm, sem):
     copies = [pltpu.make_async_copy(one, one_hbm, sem.at[0]), pltpu.make_async_copy(two, two_hbm, sem.at[1])]
     for copy in copies:
@@ -533,8 +1090,11 @@
             dma((2,)), dma((2,)), dma((2,)), dma((2,)), dma((5,)),
         ]
         field = jax.ShapeDtypeStruct(heat_source.shape, f32)
+        small = n_tm == 2 and steps == 4 and nx >= DEPTH and ny >= EDGE and ny % EDGE == 0
+        if small:
+            scratch = wide_scratch(steps, nx, ny, nz)
         one, two = pl.pallas_call(
-            functools.partial(kernel, n_tm, n_sx, n_sy),
+            functools.partial(wide_kernel, n_sx, n_sy) if small else functools.partial(kernel, n_tm, n_sx, n_sy),
             out_shape=(pltpu.VMEM(heat_source.shape, f32),) * 2,
             in_specs=[pl.BlockSpec(memory_space=pltpu.HBM)] * 3,
             out_specs=(pl.BlockSpec(memory_space=pltpu.VMEM),) * 2,

time: 38.9 us -> 34.7 us (0.89)
  Pallas kernels: 38.1 us -> 33.5 us
    pallas_call x1, Pallas kernels: 37.1 us -> 32.5 us  [per_device(): pl.pallas_call(functools.partial(wide_kernel, n_sx, n_sy) if small else f...]
where the time goes in v2:
time: 34.7 us; the launch traced here: 34.2 us
  Pallas kernels  33.5 us (97%)
  between operations  0.64 us (2%)
    pallas_call x1, Pallas kernels, per_device(): pl.pallas_call(functools.partial(wide_kernel, n_sx, n_sy) if small else f...  32.5 us
    pallas_call x1, Pallas kernels, per_device(): pl.pallas_call(store, out_shape=(field, field), in_specs=[pl.BlockSpec(me...  0.99 us

profile of v2, /device:TPU:3, one launch (start us, length us, event | category | flops | bytes accessed | tf_op | source)
XLA Modules:
  0.0 34.2 jit_solution(1402100686219281259)
XLA Ops:
  0.6 32.5 %vcycle.1 = (f32[4,16,16,128]{3,2,1,0:T(8,128)S(1)}, f32[4,16,16,128]{3,2,1,0:T(8,128)S(1)}) custom-call(f32[4,16,16,128]{3,2,1,0:T(8,128)} %hs_hbm.1, f32[16,16,128]{2,1,0:T(8,128)} %k_hbm.1, f32[4,16,16,128]{3,2,1,0:T(8,128)} %in_hbm.1), custom_call_target="tpu_custom_call" | custom-call | tf_op jit(solution)/shard_map/vcycle/pallas_call | solution.py:1096
  33.2 1.0 %store.1 = (f32[4,16,16,128]{3,2,1,0:T(8,128)}, f32[4,16,16,128]{3,2,1,0:T(8,128)}) custom-call(f32[4,16,16,128]{3,2,1,0:T(8,128)S(1)} %get-tuple-element.4.one, f32[4,16,16,128]{3,2,1,0:T(8,128)S(1)} %get-tuple-element.5.two), custom_call_target="tpu_custom_call" | custom-call | tf_op jit(solution)/shard_map/store/pallas_call | solution.py:1107

commit v3 on v2

--- a/solution.py
+++ b/solution.py
@@ -498,6 +498,7 @@
 
 DEPTH = 6
 EDGE = 8
+REACH = 4
 EXCHANGES = {
     "kappa": ("k", (0, 1), ()),
     "kappa_far": ("k", (1, 6), ((0, 5, 0, 5),)),
@@ -531,6 +532,7 @@
     at_one = jnp.where(tm > 0, 1.0, 0.0)
     at_zero = 1.0 - at_one
     mid = pl.ds(EDGE, ny)
+    win = pl.ds(EDGE - REACH, ny + 2 * REACH)
     inner = pl.ds(DEPTH, nx)
     homes = {"k": kap, "in": ini, "hs": src, "first": first, "pair": pair, "err": err,
              "last": last, "prev": prev, "rhs3": rhs3}
@@ -571,11 +573,13 @@
 
     pl.semaphore_signal(barrier, inc=1, device_id={"tm": 1 - tm}, device_id_type=MESH)
 
-    def rows(body, depth, by=4):
+    def rows(body, depth, by=None):
         def step(x, carry):
             body(x)
             return carry
 
+        if by is None:
+            by = (nx + 2 * depth) // (2 if depth else 1)
         lax.fori_loop(DEPTH - depth, DEPTH + nx + depth, step, 0, unroll=by)
 
     filled = ((kap, 6), (ini, 1), (src, 1), (first, 2), (pair, 2), (err, 5), (last, 5), (prev, 5), (rhs3, 5))
@@ -594,7 +598,7 @@
                 for t in range(array.shape[0]):
                     array[t, x, pl.ds(start, EDGE), :] = strip
 
-            rows(body, depth)
+            rows(body, depth, 2)
 
     @pl.when(sx == 0)
     def _():
@@ -619,13 +623,13 @@
             prev[0, x] = plane
             prev[1, x] = plane
 
-        rows(body, 5)
+        rows(body, 5, 2)
 
         def empty(x):
             before[x - DEPTH] = jnp.zeros((ny, nz), jnp.float32)
             ahead[x - DEPTH] = jnp.zeros((ny, nz), jnp.float32)
 
-        rows(empty, 0)
+        rows(empty, 0, 2)
 
     pl.semaphore_wait(barrier, count)
 
@@ -736,21 +740,23 @@
             pltpu.roll(here, nz - 1, 1), pltpu.roll(here, 1, 1),
         )
 
-    def around_mid(ref, t, x):
-        here = ref[t, x, mid, :]
+    def around_part(ref, t, x, size):
+        low = EDGE - (size - ny) // 2
+        part = pl.ds(low, size)
+        here = ref[t, x, part, :]
         return here, (
-            ref[t, x + 1, mid, :], ref[t, x - 1, mid, :],
-            ref[t, x, pl.ds(EDGE + 1, ny), :], ref[t, x, pl.ds(EDGE - 1, ny), :],
+            ref[t, x + 1, part, :], ref[t, x - 1, part, :],
+            ref[t, x, pl.ds(low + 1, size), :], ref[t, x, pl.ds(low - 1, size), :],
             pltpu.roll(here, nz - 1, 1), pltpu.roll(here, 1, 1),
         )
 
     def beside(ref, t, x, g):
-        here, sides = (around if g[0].shape[0] == wide else around_mid)(ref, t, x)
+        here, sides = around_part(ref, t, x, g[0].shape[0])
         terms = [g[j] * sides[j] for j in range(6)]
         return here, (terms[0] + terms[1]) + (terms[2] + terms[3]) + (terms[4] + terms[5])
 
     def faces(x):
-        return [face[j, x] for j in range(6)]
+        return [face[j, x, win, :] for j in range(6)]
 
     def faces_mid(x):
         return [face[j, x, mid, :] for j in range(6)]
@@ -767,7 +773,7 @@
         return g, whole
 
     def coefficients_mid(x):
-        g, whole = couple(*around_mid(kap, 0, x), column[:ny])
+        g, whole = couple(*around_part(kap, 0, x, ny), column[:ny])
         coupling[x, mid, :] = whole
         for j in range(6):
             face[j, x, mid, :] = g[j]
@@ -793,7 +799,7 @@
             body(x)
             return carry
 
-        lax.fori_loop(DEPTH + edge, DEPTH + nx - edge, step, 0, unroll=4)
+        lax.fori_loop(DEPTH + edge, DEPTH + nx - edge, step, 0, unroll=nx // 2 - edge)
         send(name, REST)
 
     loads[0].wait()
@@ -861,8 +867,8 @@
 
     def down_two(x):
         here, near = beside(pair, 0, x, faces(x))
-        value = 0.25 * (1.0 + 2.0 * coupling[x]) * here + 2.0 * near + pair[2, x]
-        fr[0, x] = factor[2, x] * value
+        value = 0.25 * (1.0 + 2.0 * coupling[x, win, :]) * here + 2.0 * near + pair[2, x, win, :]
+        fr[0, x, win, :] = factor[2, x, win, :] * value
 
     rows(down_two, 1)
 
@@ -916,35 +922,35 @@
     rows(gather_far, 5)
 
     def level_two(x):
-        g, f, weight = faces(x), factor[2, x], 0.25 * (1.0 + 2.0 * coupling[x])
+        g, f, weight = faces(x), factor[2, x, win, :], 0.25 * (1.0 + 2.0 * coupling[x, win, :])
         here, near = beside(sums, 0, x, g)
-        err2[0, x] = f * (weight * here + 2.0 * near + prev[1, x])
+        err2[0, x, win, :] = f * (weight * here + 2.0 * near + prev[1, x, win, :])
         here, near = beside(sums, 1, x, g)
-        err2[1, x] = f * (weight * here + 2.0 * near)
+        err2[1, x, win, :] = f * (weight * here + 2.0 * near)
 
     rows(level_two, 4)
 
     def own_errors(x):
-        f = factor[1, x]
-        carried = f * last[0, x]
-        return err[0, x] + carried, err[1, x] + f * carried
+        f = factor[1, x, win, :]
+        carried = f * last[0, x, win, :]
+        return err[0, x, win, :] + carried, err[1, x, win, :] + f * carried
 
     def fix_two(x):
-        g, f = faces(x), factor[2, x]
+        g, f = faces(x), factor[2, x, win, :]
         own, near = beside(err2, 0, x, g)
         past, near_past = beside(err2, 1, x, g)
         value = (2.0 - relax_weight) * own + f * (4.0 * near + past)
         value_past = (2.0 - relax_weight) * past + 4.0 * (f * near_past)
         zero, first_one = own_errors(x)
-        fix[0, x] = zero + value
-        fix[1, x] = first_one + value
-        fix[2, x] = prev[0, x] + value_past
-        fix[3, x] = prev[1, x] + value_past
+        fix[0, x, win, :] = zero + value
+        fix[1, x, win, :] = first_one + value
+        fix[2, x, win, :] = prev[0, x, win, :] + value_past
+        fix[3, x, win, :] = prev[1, x, win, :] + value_past
 
     rows(fix_two, 3)
 
     def fix_one(x):
-        g, f = faces(x), factor[1, x]
+        g, f = faces(x), factor[1, x, win, :]
         here, near = [], []
         for i in range(4):
             a, b = beside(fix, i, x, g)
@@ -952,11 +958,11 @@
             near.append(keep_weight * a + 2.0 * (f * b))
         zero, first_one = own_errors(x)
         value = near[0] + zero + f * here[3]
-        vee[0, x] = value
-        vee[1, x] = near[1] + first_one + f * (value - zero)
-        value = near[2] + prev[0, x]
-        vee[2, x] = value
-        vee[3, x] = near[3] + prev[1, x] + f * (value - prev[0, x])
+        vee[0, x, win, :] = value
+        vee[1, x, win, :] = near[1] + first_one + f * (value - zero)
+        value = near[2] + prev[0, x, win, :]
+        vee[2, x, win, :] = value
+        vee[3, x, win, :] = near[3] + prev[1, x, win, :] + f * (value - prev[0, x, win, :])
 
     rows(fix_one, 2)
     wait("rhs3")
@@ -968,42 +974,42 @@
 
     def coarse_two(x):
         here, near = beside(one, 0, x, faces(x))
-        err3[0, x] = keep_weight * here + factor[3, x] * (rhs3[0, x] + 8.0 * near)
+        err3[0, x, win, :] = keep_weight * here + factor[3, x, win, :] * (rhs3[0, x, win, :] + 8.0 * near)
 
     rows(coarse_two, 4)
 
     def up_two(x):
-        f = factor[2, x]
+        f = factor[2, x, win, :]
         here, near = beside(err3, 0, x, faces(x))
         value = keep_weight * here + 4.0 * (f * near)
-        wave[0, x] = value + at_one * (f * here)
-        wave[1, x] = value
+        wave[0, x, win, :] = value + at_one * (f * here)
+        wave[1, x, win, :] = value
 
     rows(up_two, 3)
 
     def up_one(x):
-        g, f = faces(x), factor[1, x]
+        g, f = faces(x), factor[1, x, win, :]
         here, near = beside(wave, 0, x, g)
         past, near_past = beside(wave, 1, x, g)
         own = keep_weight * here + 2.0 * (f * near)
         shadow = at_one * (keep_weight * past + 2.0 * (f * near_past))
         zero = own + at_one * (f * past)
-        gain = (vee[0, x] + zero, vee[1, x] + own + f * zero)
+        gain = (vee[0, x, win, :] + zero, vee[1, x, win, :] + own + f * zero)
         for t in range(steps):
-            total[t, x] = first[t, x] + gain[t // 2]
-        vee[2, x] = vee[2, x] + shadow
-        vee[3, x] = vee[3, x] + shadow + f * shadow
+            total[t, x, win, :] = first[t, x, win, :] + gain[t // 2]
+        vee[2, x, win, :] = vee[2, x, win, :] + shadow
+        vee[3, x, win, :] = vee[3, x, win, :] + shadow + f * shadow
 
     rows(up_one, 2)
     wait("source")
 
     def up_zero(x):
-        g, f = faces(x), factor[0, x]
-        running = last[0, x] + vee[3, x]
+        g, f = faces(x), factor[0, x, win, :]
+        running = last[0, x, win, :] + vee[3, x, win, :]
         for t in range(steps):
             here, near = beside(total, t, x, g)
-            running = keep_weight * here + f * (src[t, x] + near + running)
-            sol[t, x] = running
+            running = keep_weight * here + f * (src[t, x, win, :] + near + running)
+            sol[t, x, win, :] = running
 
     rows(up_zero, 1)
     arrive(T_GUESS)

time: 34.7 us -> 32.2 us (0.928)
  Pallas kernels: 33.5 us -> 31.2 us
    pallas_call x1, Pallas kernels: 32.5 us -> 30.2 us  [per_device(): pl.pallas_call(functools.partial(wide_kernel, n_sx, n_sy) if small else f...]
where the time goes in v3:
time: 32.2 us; the launch traced here: 31.8 us
  Pallas kernels  31.2 us (97%)
  between operations  0.64 us (2%)
    pallas_call x1, Pallas kernels, per_device(): pl.pallas_call(functools.partial(wide_kernel, n_sx, n_sy) if small else f...  30.2 us
    pallas_call x1, Pallas kernels, per_device(): pl.pallas_call(store, out_shape=(field, field), in_specs=[pl.BlockSpec(me...  0.99 us

profile of v3, /device:TPU:3, one launch (start us, length us, event | category | flops | bytes accessed | tf_op | source)
XLA Modules:
  0.0 31.8 jit_solution(12381565134003661114)
XLA Ops:
  0.6 30.2 %vcycle.1 = (f32[4,16,16,128]{3,2,1,0:T(8,128)S(1)}, f32[4,16,16,128]{3,2,1,0:T(8,128)S(1)}) custom-call(f32[4,16,16,128]{3,2,1,0:T(8,128)} %hs_hbm.1, f32[16,16,128]{2,1,0:T(8,128)} %k_hbm.1, f32[4,16,16,128]{3,2,1,0:T(8,128)} %in_hbm.1), custom_call_target="tpu_custom_call" | custom-call | tf_op jit(solution)/shard_map/vcycle/pallas_call | solution.py:1102
  30.8 1.0 %store.1 = (f32[4,16,16,128]{3,2,1,0:T(8,128)}, f32[4,16,16,128]{3,2,1,0:T(8,128)}) custom-call(f32[4,16,16,128]{3,2,1,0:T(8,128)S(1)} %get-tuple-element.4.one, f32[4,16,16,128]{3,2,1,0:T(8,128)S(1)} %get-tuple-element.5.two), custom_call_target="tpu_custom_call" | custom-call | tf_op jit(solution)/shard_map/store/pallas_call | solution.py:1113

commit v4 on v3

--- a/solution.py
+++ b/solution.py
@@ -536,7 +536,6 @@
     inner = pl.ds(DEPTH, nx)
     homes = {"k": kap, "in": ini, "hs": src, "first": first, "pair": pair, "err": err,
              "last": last, "prev": prev, "rhs3": rhs3}
-    outside = {"k": k_hbm, "in": in_hbm, "hs": hs_hbm}
 
     loads = [
         pltpu.make_async_copy(k_hbm, kap.at[0, inner, mid], local.at[0]),
@@ -657,13 +656,10 @@
         fy, wy, ty = span(way[1], ny, box[2], box[3])
         steps_at = {"prev_zero": pl.ds(0, 1), "prev_one": pl.ds(1, 1)}.get(name, slice(None))
         if kind == "k":
-            source = k_hbm.at[pl.ds(fx, wx), pl.ds(fy, wy)]
+            source = land.at[0, pl.ds(DEPTH + fx, wx), pl.ds(EDGE + fy, wy)]
             dest = land.at[0, pl.ds(DEPTH + tx, wx), pl.ds(EDGE + ty, wy)]
         else:
-            if kind in outside:
-                source = outside[kind].at[:, pl.ds(fx, wx), pl.ds(fy, wy)]
-            else:
-                source = land.at[steps_at, pl.ds(DEPTH + fx, wx), pl.ds(EDGE + fy, wy)]
+            source = land.at[steps_at, pl.ds(DEPTH + fx, wx), pl.ds(EDGE + fy, wy)]
             dest = land.at[steps_at, pl.ds(DEPTH + tx, wx), pl.ds(EDGE + ty, wy)]
         number = NAMES.index(name)
         return pltpu.make_async_remote_copy(
@@ -690,12 +686,13 @@
 
     half = nx // 2
     ends = ((0, half), (half, nx - half))
+    thirds = ((0, DEPTH - 1), (nx - DEPTH + 1, DEPTH - 1), (DEPTH - 1, nx - 2 * DEPTH + 2))
 
     def across(which, part):
-        low, size = ends[part]
+        low, size = (thirds if which == T_MINE else ends)[part]
         near, far = pl.ds(low, size), pl.ds(DEPTH + low, size)
         source, dest = {
-            T_INIT: lambda: (in_hbm.at[steps - 1, near], before.at[near]),
+            T_INIT: lambda: (ini.at[steps - 1, far, mid], before.at[near]),
             T_LAST: lambda: (first.at[steps - 1, far, mid], last.at[0, far, mid]),
             T_ONE: lambda: (err.at[1, far, mid], prev.at[1, far, mid]),
             T_ZERO: lambda: (err.at[0, far, mid], prev.at[0, far, mid]),
@@ -718,9 +715,12 @@
             for part in parts:
                 across(which, part).wait_recv()
 
+    loads[0].wait()
     send("kappa")
+    loads[1].wait()
     send("init")
     pass_on(T_INIT)
+    loads[2].wait()
     send("source")
     send("kappa_far")
 
@@ -802,11 +802,8 @@
         lax.fori_loop(DEPTH + edge, DEPTH + nx - edge, step, 0, unroll=nx // 2 - edge)
         send(name, REST)
 
-    loads[0].wait()
     wait("kappa")
     rows(coefficients_mid, 0)
-    loads[1].wait()
-    loads[2].wait()
     wait("init")
     arrive(T_INIT)
 
@@ -880,9 +877,18 @@
         base = factor[2, x, mid, :] * (0.25 * (1.0 + 2.0 * c) * here + 2.0 * near)
         mine[x - DEPTH] = value + at_zero * base
 
-    rows(down_three, 0)
-    across(T_MINE, 0).start()
-    across(T_MINE, 1).start()
+    def part_rows(body, part):
+        low, size = thirds[part]
+
+        def step(x, carry):
+            body(x)
+            return carry
+
+        lax.fori_loop(DEPTH + low, DEPTH + low + size, step, 0, unroll=size)
+
+    for part in range(3):
+        part_rows(down_three, part)
+        across(T_MINE, part).start()
     pass_on(T_GUESS)
     arrive(T_ONE)
 
@@ -896,14 +902,16 @@
     def _():
         send("prev_zero")
 
-    across(T_MINE, 0).wait_recv()
-    across(T_MINE, 1).wait_recv()
-
     def add_up(x):
         rhs3[0, x, mid, :] = mine[x - DEPTH] + theirs[x - DEPTH]
 
-    rows(add_up, 0)
-    send("rhs3")
+    for part in range(2):
+        across(T_MINE, part).wait_recv()
+        part_rows(add_up, part)
+        send("rhs3", ((2 * part - 1, 0), (2 * part - 1, -1), (2 * part - 1, 1)))
+    across(T_MINE, 2).wait_recv()
+    part_rows(add_up, 2)
+    send("rhs3", ((0, -1), (0, 1)))
 
     wait("err")
     wait("first_far")
@@ -1044,8 +1052,8 @@
             for part in range(2):
                 across(which, part).wait_send()
 
-    across(T_MINE, 0).wait_send()
-    across(T_MINE, 1).wait_send()
+    for part in range(3):
+        across(T_MINE, part).wait_send()
 
 
 def wide_scratch(steps, nx, ny, nz):
@@ -1055,7 +1063,7 @@
     scratch = [pltpu.VMEM((d,) + large, f32) for d in depths]
     scratch += [pltpu.VMEM(large, f32), pltpu.VMEM((4,) + large, f32)]
     scratch += [pltpu.VMEM((nx, ny, nz), f32)] * 5
-    scratch += [dma((len(NAMES), 12)), dma((len(NAMES), 12)), dma((6, 2)), dma((6, 2)), dma((3,))]
+    scratch += [dma((len(NAMES), 12)), dma((len(NAMES), 12)), dma((6, 3)), dma((6, 3)), dma((3,))]
     return scratch
 
 
@@ -1096,7 +1104,7 @@
             dma((2,)), dma((2,)), dma((2,)), dma((2,)), dma((5,)),
         ]
         field = jax.ShapeDtypeStruct(heat_source.shape, f32)
-        small = n_tm == 2 and steps == 4 and nx >= DEPTH and ny >= EDGE and ny % EDGE == 0
+        small = n_tm == 2 and steps == 4 and nx >= 2 * DEPTH and ny >= EDGE and ny % EDGE == 0
         if small:
             scratch = wide_scratch(steps, nx, ny, nz)
         one, two = pl.pallas_call(

time: 32.2 us -> 31.2 us (0.969)
  Pallas kernels: 31.2 us -> 30.3 us
    pallas_call x1, Pallas kernels: 30.2 us -> 29.3 us  [per_device(): pl.pallas_call(functools.partial(wide_kernel, n_sx, n_sy) if small else f...]
where the time goes in v4:
time: 31.2 us; the launch traced here: 30.9 us
  Pallas kernels  30.3 us (97%)
  between operations  0.64 us (2%)
    pallas_call x1, Pallas kernels, per_device(): pl.pallas_call(functools.partial(wide_kernel, n_sx, n_sy) if small else f...  29.3 us
    pallas_call x1, Pallas kernels, per_device(): pl.pallas_call(store, out_shape=(field, field), in_specs=[pl.BlockSpec(me...  0.99 us

profile of v4, /device:TPU:3, one launch (start us, length us, event | category | flops | bytes accessed | tf_op | source)
XLA Modules:
  0.0 30.9 jit_solution(8323481795004542902)
XLA Ops:
  0.6 29.3 %vcycle.1 = (f32[4,16,16,128]{3,2,1,0:T(8,128)S(1)}, f32[4,16,16,128]{3,2,1,0:T(8,128)S(1)}) custom-call(f32[4,16,16,128]{3,2,1,0:T(8,128)} %hs_hbm.1, f32[16,16,128]{2,1,0:T(8,128)} %k_hbm.1, f32[4,16,16,128]{3,2,1,0:T(8,128)} %in_hbm.1), custom_call_target="tpu_custom_call" | custom-call | tf_op jit(solution)/shard_map/vcycle/pallas_call | solution.py:1110
  30.0 1.0 %store.1 = (f32[4,16,16,128]{3,2,1,0:T(8,128)}, f32[4,16,16,128]{3,2,1,0:T(8,128)}) custom-call(f32[4,16,16,128]{3,2,1,0:T(8,128)S(1)} %get-tuple-element.4.one, f32[4,16,16,128]{3,2,1,0:T(8,128)S(1)} %get-tuple-element.5.two), custom_call_target="tpu_custom_call" | custom-call | tf_op jit(solution)/shard_map/store/pallas_call | solution.py:1121

commit v5 on v4

--- a/solution.py
+++ b/solution.py
@@ -973,6 +973,24 @@
         vee[3, x, win, :] = near[3] + prev[1, x, win, :] + f * (value - prev[0, x, win, :])
 
     rows(fix_one, 2)
+    for name in NAMES:
+        if name in ("last", "prev_one", "prev_zero"):
+            @pl.when(tm > 0)
+            def _(name=name):
+                wait_sent(name)
+        elif name != "rhs3":
+            wait_sent(name)
+
+    @pl.when(tm == 0)
+    def _():
+        for which in (T_INIT, T_LAST, T_ONE, T_ZERO):
+            for part in range(2):
+                across(which, part).wait_send()
+
+    for part in range(3):
+        across(T_MINE, part).wait_send()
+
+    wait("source")
     wait("rhs3")
 
     def coarse_one(x):
@@ -1009,7 +1027,6 @@
         vee[3, x, win, :] = vee[3, x, win, :] + shadow + f * shadow
 
     rows(up_one, 2)
-    wait("source")
 
     def up_zero(x):
         g, f = faces(x), factor[0, x, win, :]
@@ -1038,22 +1055,12 @@
 
     rows(finish, 0)
 
-    for name in NAMES:
-        if name in ("last", "prev_one", "prev_zero"):
-            @pl.when(tm > 0)
-            def _(name=name):
-                wait_sent(name)
-        else:
-            wait_sent(name)
+    wait_sent("rhs3")
 
     @pl.when(tm == 0)
     def _():
-        for which in (T_INIT, T_LAST, T_ONE, T_ZERO, T_GUESS):
-            for part in range(2):
-                across(which, part).wait_send()
-
-    for part in range(3):
-        across(T_MINE, part).wait_send()
+        for part in range(2):
+            across(T_GUESS, part).wait_send()
 
 
 def wide_scratch(steps, nx, ny, nz):

time: 31.2 us -> 31.1 us (level)
  no operation moved by 1% of the time
where the time goes in v5:
time: 31.1 us; the launch traced here: 30.9 us
  Pallas kernels  30.3 us (97%)
  between operations  0.64 us (2%)
    pallas_call x1, Pallas kernels, per_device(): pl.pallas_call(functools.partial(wide_kernel, n_sx, n_sy) if small else f...  29.3 us
    pallas_call x1, Pallas kernels, per_device(): pl.pallas_call(store, out_shape=(field, field), in_specs=[pl.BlockSpec(me...  0.99 us

profile of v5, /device:TPU:3, one launch (start us, length us, event | category | flops | bytes accessed | tf_op | source)
XLA Modules:
  0.0 30.9 jit_solution(16530199001763429831)
XLA Ops:
  0.6 29.3 %vcycle.1 = (f32[4,16,16,128]{3,2,1,0:T(8,128)S(1)}, f32[4,16,16,128]{3,2,1,0:T(8,128)S(1)}) custom-call(f32[4,16,16,128]{3,2,1,0:T(8,128)} %hs_hbm.1, f32[16,16,128]{2,1,0:T(8,128)} %k_hbm.1, f32[4,16,16,128]{3,2,1,0:T(8,128)} %in_hbm.1), custom_call_target="tpu_custom_call" | custom-call | tf_op jit(solution)/shard_map/vcycle/pallas_call | solution.py:1117
  30.0 1.0 %store.1 = (f32[4,16,16,128]{3,2,1,0:T(8,128)}, f32[4,16,16,128]{3,2,1,0:T(8,128)}) custom-call(f32[4,16,16,128]{3,2,1,0:T(8,128)S(1)} %get-tuple-element.4.one, f32[4,16,16,128]{3,2,1,0:T(8,128)S(1)} %get-tuple-element.5.two), custom_call_target="tpu_custom_call" | custom-call | tf_op jit(solution)/shard_map/store/pallas_call | solution.py:1128

commit v6 on v5

--- a/solution.py
+++ b/solution.py
@@ -507,6 +507,7 @@
     "first": ("first", (0, 1), ()),
     "first_far": ("first", (1, 2), ((0, 1, 0, 1),)),
     "pair": ("pair", (0, 2), ((0, 1, 0, 1),)),
+    "pair_near": ("pair", (0, 1), ()),
     "err": ("err", (0, 5), ((0, 4, 0, 4),)),
     "last": ("last", (0, 5), ((0, 4, 0, 4),)),
     "prev_one": ("prev", (0, 5), ((0, 4, 0, 4),)),
@@ -654,7 +655,8 @@
         land = homes[kind]
         fx, wx, tx = span(way[0], nx, box[0], box[1])
         fy, wy, ty = span(way[1], ny, box[2], box[3])
-        steps_at = {"prev_zero": pl.ds(0, 1), "prev_one": pl.ds(1, 1)}.get(name, slice(None))
+        steps_at = {"prev_zero": pl.ds(0, 1), "prev_one": pl.ds(1, 1),
+                    "pair": pl.ds(0, 1), "pair_near": pl.ds(1, 2)}.get(name, slice(None))
         if kind == "k":
             source = land.at[0, pl.ds(DEPTH + fx, wx), pl.ds(EDGE + fy, wy)]
             dest = land.at[0, pl.ds(DEPTH + tx, wx), pl.ds(EDGE + ty, wy)]
@@ -789,18 +791,27 @@
         for level in range(4):
             factor[level, x] = jnp.where(inside, relax_weight / (1.0 + (2.0 ** level) * whole), 0.0)
 
-    def phase(body, edge, name):
+    def phase(body, edge, name, passing=()):
         for i in range(edge):
             body(DEPTH + i)
             body(DEPTH + nx - 1 - i)
-        send(name, X_FACES)
+        names = (name, "pair_near") if name == "pair" else (name,)
+        for each in names:
+            send(each, X_FACES)
 
         def step(x, carry):
             body(x)
             return carry
 
-        lax.fori_loop(DEPTH + edge, DEPTH + nx - edge, step, 0, unroll=nx // 2 - edge)
-        send(name, REST)
+        if passing:
+            for part, (low, high) in enumerate(((edge, half), (half, nx - edge))):
+                lax.fori_loop(DEPTH + low, DEPTH + high, step, 0, unroll=high - low)
+                for which in passing:
+                    pass_on(which, (part,))
+        else:
+            lax.fori_loop(DEPTH + edge, DEPTH + nx - edge, step, 0, unroll=nx // 2 - edge)
+        for each in names:
+            send(each, REST)
 
     wait("kappa")
     rows(coefficients_mid, 0)
@@ -850,9 +861,7 @@
         pair[2, x, mid, :] = at_zero * running
         guess[x - DEPTH] = ahead_value
 
-    phase(down_one, 2, "pair")
-    pass_on(T_ONE)
-    pass_on(T_ZERO)
+    phase(down_one, 2, "pair", (T_ONE, T_ZERO))
     send("err")
     arrive(T_LAST)
 
@@ -861,6 +870,7 @@
         send("last")
 
     wait("pair")
+    wait("pair_near")
 
     def down_two(x):
         here, near = beside(pair, 0, x, faces(x))
@@ -1075,7 +1085,11 @@
 
 
 def store(one, two, one_hbm, two_hbm, sem):
-    copies = [pltpu.make_async_copy(one, one_hbm, sem.at[0]), pltpu.make_async_copy(two, two_hbm, sem.at[1])]
+    copies = [
+        pltpu.make_async_copy(held.at[t], hbm.at[t], sem.at[i, t])
+        for i, (held, hbm) in enumerate(((one, one_hbm), (two, two_hbm)))
+        for t in range(one.shape[0])
+    ]
     for copy in copies:
         copy.start()
     for copy in copies:
@@ -1130,7 +1144,7 @@
             out_shape=(field, field),
             in_specs=[pl.BlockSpec(memory_space=pltpu.VMEM)] * 2,
             out_specs=(pl.BlockSpec(memory_space=pltpu.HBM),) * 2,
-            scratch_shapes=[dma((2,))],
+            scratch_shapes=[dma((2, steps))],
             name="store",
         )(*(pltpu.with_memory_space_constraint(x, pltpu.VMEM) for x in (one, two)))
 

time: 31.1 us -> 31.1 us (level)
  no operation moved by 1% of the time
where the time goes in v6:
time: 31.1 us; the launch traced here: 31 us
  Pallas kernels  30.4 us (98%)
  between operations  0.64 us (2%)
    pallas_call x1, Pallas kernels, per_device(): pl.pallas_call(functools.partial(wide_kernel, n_sx, n_sy) if small else f...  29.3 us
    pallas_call x1, Pallas kernels, per_device(): pl.pallas_call(store, out_shape=(field, field), in_specs=[pl.BlockSpec(me...  1.03 us

profile of v6, /device:TPU:3, one launch (start us, length us, event | category | flops | bytes accessed | tf_op | source)
XLA Modules:
  0.0 31.0 jit_solution(5660773018245098915)
XLA Ops:
  0.6 29.3 %vcycle.1 = (f32[4,16,16,128]{3,2,1,0:T(8,128)S(1)}, f32[4,16,16,128]{3,2,1,0:T(8,128)S(1)}) custom-call(f32[4,16,16,128]{3,2,1,0:T(8,128)} %hs_hbm.1, f32[16,16,128]{2,1,0:T(8,128)} %k_hbm.1, f32[4,16,16,128]{3,2,1,0:T(8,128)} %in_hbm.1), custom_call_target="tpu_custom_call" | custom-call | tf_op jit(solution)/shard_map/vcycle/pallas_call | solution.py:1131
  30.0 1.0 %store.1 = (f32[4,16,16,128]{3,2,1,0:T(8,128)}, f32[4,16,16,128]{3,2,1,0:T(8,128)}) custom-call(f32[4,16,16,128]{3,2,1,0:T(8,128)S(1)} %get-tuple-element.4.one, f32[4,16,16,128]{3,2,1,0:T(8,128)S(1)} %get-tuple-element.5.two), custom_call_target="tpu_custom_call" | custom-call | tf_op jit(solution)/shard_map/store/pallas_call | solution.py:1142

commit v7 on v5

--- a/solution.py
+++ b/solution.py
@@ -1075,7 +1075,11 @@
 
 
 def store(one, two, one_hbm, two_hbm, sem):
-    copies = [pltpu.make_async_copy(one, one_hbm, sem.at[0]), pltpu.make_async_copy(two, two_hbm, sem.at[1])]
+    copies = [
+        pltpu.make_async_copy(held.at[t], hbm.at[t], sem.at[i, t])
+        for i, (held, hbm) in enumerate(((one, one_hbm), (two, two_hbm)))
+        for t in range(one.shape[0])
+    ]
     for copy in copies:
         copy.start()
     for copy in copies:
@@ -1130,7 +1134,7 @@
             out_shape=(field, field),
             in_specs=[pl.BlockSpec(memory_space=pltpu.VMEM)] * 2,
             out_specs=(pl.BlockSpec(memory_space=pltpu.HBM),) * 2,
-            scratch_shapes=[dma((2,))],
+            scratch_shapes=[dma((2, steps))],
             name="store",
         )(*(pltpu.with_memory_space_constraint(x, pltpu.VMEM) for x in (one, two)))
 

time: 31.1 us -> 31.1 us (level)
  no operation moved by 1% of the time
where the time goes in v7:
time: 31.1 us; the launch traced here: 31 us
  Pallas kernels  30.3 us (97%)
  between operations  0.64 us (2%)
    pallas_call x1, Pallas kernels, per_device(): pl.pallas_call(functools.partial(wide_kernel, n_sx, n_sy) if small else f...  29.3 us
    pallas_call x1, Pallas kernels, per_device(): pl.pallas_call(store, out_shape=(field, field), in_specs=[pl.BlockSpec(me...  1.03 us

profile of v7, /device:TPU:3, one launch (start us, length us, event | category | flops | bytes accessed | tf_op | source)
XLA Modules:
  0.0 31.0 jit_solution(1926565866294801084)
XLA Ops:
  0.6 29.3 %vcycle.1 = (f32[4,16,16,128]{3,2,1,0:T(8,128)S(1)}, f32[4,16,16,128]{3,2,1,0:T(8,128)S(1)}) custom-call(f32[4,16,16,128]{3,2,1,0:T(8,128)} %hs_hbm.1, f32[16,16,128]{2,1,0:T(8,128)} %k_hbm.1, f32[4,16,16,128]{3,2,1,0:T(8,128)} %in_hbm.1), custom_call_target="tpu_custom_call" | custom-call | tf_op jit(solution)/shard_map/vcycle/pallas_call | solution.py:1121
  30.0 1.0 %store.1 = (f32[4,16,16,128]{3,2,1,0:T(8,128)}, f32[4,16,16,128]{3,2,1,0:T(8,128)}) custom-call(f32[4,16,16,128]{3,2,1,0:T(8,128)S(1)} %get-tuple-element.4.one, f32[4,16,16,128]{3,2,1,0:T(8,128)S(1)} %get-tuple-element.5.two), custom_call_target="tpu_custom_call" | custom-call | tf_op jit(solution)/shard_map/store/pallas_call | solution.py:1132
